TPU v7x, 32 devices: a whole 2x2x4 slice. The times are simulated.
32 devices in a mesh: groups: 2 (over x), space: 16 (over z, y, core).
Axes of the slice: x: 2, y: 2, z: 4, core: 2. Of those that a mesh axis runs over, the one named last changes fastest.
Arguments:
- grid_in: bfloat16 [96, 1440, 128], P(('groups', 'space')), parts along dimension 0, may hold values from -6 to 6
- upstream: bfloat16 [96, 1440, 128], P(('groups', 'space')), parts along dimension 0, may hold values from -6 to 6
- mix_weight: bfloat16 [2, 128, 128], replicated, may hold values from -0.375 to 0.375
- degree_filter: bfloat16 [512, 128], replicated, may hold values from 0.25 to 2
Outputs:
- grad_in: bfloat16 [96, 1440, 128], P(('groups', 'space')), parts along dimension 0
- grad_weight: float32 [4, 128, 128], P('groups'), parts along dimension 0
- grad_filter: float32 [1024, 128], P('groups'), parts along dimension 0
There are 2 independent parts, one for each index of `groups`. A program takes and returns all parts, laid end to end along the dimension named above; an argument that names none is the same for every part. Nothing has to cross between parts.
All inputs are finite; a program needn't handle non-finite values.
Results may differ from a plain program's by a relative error of at most 0.02.
Values may be sent and summed in bfloat16 or wider, within the bound.
A program may use at most 128 MiB of HBM per device.

v0:
```python
import functools
import math

import jax
import jax.numpy as jnp
import numpy as np
from jax import lax
from jax.experimental import pallas as pl
from jax.experimental.pallas import tpu as pltpu
from jax.sharding import PartitionSpec as P

MODES = 512
ROWS = 32
F32 = jnp.float32
BF16 = jnp.bfloat16


def params(**extra):
    return pltpu.CompilerParams(vmem_limit_bytes=56 * 1024 * 1024, **extra)


def latitude_angles(index, lat_count):
    return math.pi * (index.astype(F32) + 0.5) / lat_count


def greet(devices):
    me = lax.axis_index("space")
    barrier = pltpu.get_barrier_semaphore()

    def hello(step, carry):
        peer = (me + step) % devices
        pl.semaphore_signal(
            barrier, inc=1, device_id={"space": peer}, device_id_type=pl.DeviceIdType.MESH
        )
        return carry

    lax.fori_loop(1, devices, hello, 0)


def await_greetings(devices):
    pl.semaphore_wait(pltpu.get_barrier_semaphore(), devices - 1)


def remote(src, dst, send_sem, recv_sem, peer):
    return pltpu.make_async_remote_copy(
        src_ref=src,
        dst_ref=dst,
        send_sem=send_sem,
        recv_sem=recv_sem,
        device_id={"space": peer},
        device_id_type=pl.DeviceIdType.MESH,
    )


class Exchange:
    def __init__(self, source, target, send_sem, recv_sem):
        self.source, self.target = source, target
        self.send_sem, self.recv_sem = send_sem, recv_sem
        self.devices = source.shape[1]
        self.me = lax.axis_index("space")

    def copy(self, section, step):
        peer = (self.me + step) % self.devices
        return remote(
            self.source.at[section, peer],
            self.target.at[section, self.me],
            self.send_sem.at[section, step],
            self.recv_sem.at[section, step],
            peer,
        )

    def send(self, section):
        half = self.devices // 2

        def one(index, carry):
            sign = 1 - 2 * (index % 2)
            step = (half + sign * ((index + 1) // 2) + self.devices) % self.devices
            self.copy(section, step).start()
            return carry

        lax.fori_loop(0, self.devices - 1, one, 0)
        self.target[section, self.me] = self.source[section, self.me]

    def arrive(self, section):
        def one(step, carry):
            self.copy(section, step).wait_recv()
            return carry

        lax.fori_loop(1, self.devices, one, 0)

    def drain(self):
        for section in range(self.source.shape[0]):

            def one(step, carry, section=section):
                self.copy(section, step).wait_send()
                return carry

            lax.fori_loop(1, self.devices, one, 0)


class Reduction:
    def __init__(self, red, inbox, total, send_sem, recv_sem):
        self.red, self.inbox, self.total = red, inbox, total
        self.send_sem, self.recv_sem = send_sem, recv_sem
        devices = red.shape[0]
        me = lax.axis_index("space")
        self.hops = []
        base = me * 0
        stride = 1
        while stride < devices:
            half = devices // (2 * stride)
            bit = me // stride % 2
            keep, give = base + bit * half, base + (1 - bit) * half
            self.hops.append((half, keep, give, me + (1 - 2 * bit) * stride))
            base = keep
            stride *= 2
        self.base = base

    def scatter(self, held):
        count = len(self.hops)
        early = max(1, len(held) - 2) if held else 0
        for send in held[:early]:
            send()
        late = held[early:]
        for t, (half, keep, give, partner) in enumerate(self.hops):
            copy = remote(
                self.red.at[pl.ds(give, half)],
                self.inbox.at[pl.ds(half, half)],
                self.send_sem.at[t],
                self.recv_sem.at[t],
                partner,
            )
            copy.start()
            index = t - (count - len(late))
            if index >= 0:
                late[index]()
            copy.wait()
            self.red[pl.ds(keep, half)] += self.inbox[half : 2 * half]
        self.total[pl.ds(self.base, 1)] = self.red[pl.ds(self.base, 1)]

    def gather(self, index):
        count = len(self.hops)
        t = count - 1 - index
        half, keep, _, partner = self.hops[t]
        block = self.total.at[pl.ds(keep, half)]
        copy = remote(
            block, block, self.send_sem.at[count + t], self.recv_sem.at[count + t], partner
        )
        copy.start()
        return copy


def sections_of(devices):
    return max(1, min(4, MODES // devices // 8))


def row_phase(rows, devices, lon_count):
    span = 2 * MODES // devices // sections_of(devices)
    section = rows // (span * devices)
    device = rows // span % devices
    part = rows // (span // 2) % 2
    slot = section * (span // 2) + rows % (span // 2)
    return slot * devices + device, part * (lon_count // 4)


def cosine_of(phase, lon_count):
    turn = phase - jnp.floor(phase * (1.0 / lon_count)) * lon_count
    x = (lon_count / 4 - jnp.abs(turn - lon_count / 2)) * (2.0 * math.pi / lon_count)
    y = x * x
    tail = 1.0 / 362880.0 - y * (1.0 / 39916800.0)
    tail = 1.0 / 120.0 + y * (-1.0 / 5040.0 + y * tail)
    return -x * (1.0 + y * (-1.0 / 6.0 + y * tail))


def angle_indices(devices, lon_count):
    order, offset = row_phase(np.arange(2 * MODES), devices, lon_count)

    def column(values):
        return np.broadcast_to(values.astype(np.float32)[:, None], (len(values), 128))

    def lanes(values):
        return np.broadcast_to(values.astype(np.float32)[None, :], (8, len(values)))

    columns = np.stack([column(v) for v in (order[::ROWS], offset[::ROWS], order[:ROWS], offset[:ROWS])])
    return jnp.asarray(columns), jnp.asarray(np.stack([lanes(order), lanes(offset)]))


def angles_by_row(columns, lon_count, big, small):
    rows = big.shape[1]
    lon = lax.broadcasted_iota(jnp.int32, (rows, lon_count), 1).astype(F32)
    phase = columns[0][:, 0:1] * lon + columns[1][:, 0:1]
    big[0] = cosine_of(phase, lon_count)
    big[1] = cosine_of(phase + 0.75 * lon_count, lon_count)
    lon = lax.broadcasted_iota(jnp.int32, (ROWS, lon_count), 1).astype(F32)
    phase = columns[2][:, 0:1] * lon + columns[3][:, 0:1]
    factor = 1.0 / math.sqrt(lon_count)
    small[0] = cosine_of(phase, lon_count) * factor
    small[1] = cosine_of(phase + 0.75 * lon_count, lon_count) * factor


def angles_by_lane(lanes, lon_count, big, small):
    rows, total = big.shape[1:]
    order, offset = lanes[0, 0:1, :], lanes[1, 0:1, :]
    lon = lax.broadcasted_iota(jnp.int32, (rows, total), 0).astype(F32) * float(ROWS)
    phase = lon * order
    big[0] = cosine_of(phase, lon_count)
    big[1] = cosine_of(phase + 0.75 * lon_count, lon_count)
    lon = lax.broadcasted_iota(jnp.int32, (ROWS, total), 0).astype(F32)
    phase = lon * order + offset
    factor = 1.0 / math.sqrt(lon_count)
    small[0] = cosine_of(phase, lon_count) * factor
    small[1] = cosine_of(phase + 0.75 * lon_count, lon_count) * factor


def fill(dst, big, small, count):
    def step(h, carry):
        value = big[0, pl.ds(h, 1), :] * small[0] - big[1, pl.ds(h, 1), :] * small[1]
        dst[pl.ds(pl.multiple_of(h * ROWS, ROWS), ROWS), :] = value.astype(BF16)
        return carry

    lax.fori_loop(0, count, step, 0)


def alpha_column(section, rows, span):
    row = lax.broadcasted_iota(jnp.int32, (rows, 128), 0)
    zero = jnp.logical_or(row == 0, row == span // 2)
    alpha = jnp.where(zero, 1.0, 2.0) if section == 0 else jnp.full((rows, 128), 2.0, F32)
    return alpha[:, 0:1]


def section_product(table, wide, out, section, scaled):
    _, devices, span, width = out.shape
    count = devices * span
    chunk = 256
    each = chunk // span
    for q in range(count // chunk):
        first = section * count + q * chunk
        value = jnp.dot(table[first : first + chunk, :], wide, preferred_element_type=F32)
        if scaled:
            value = value * (alpha_column(0, chunk, span) if first == 0 else 2.0)
        out[section, q * each : (q + 1) * each] = value.astype(BF16).reshape(each, span, width)


def legendre_tables(
    slot_ref, start_ref, lat_ref, synth, anal, tsynth, tanal, hold
):
    groups, width = slot_ref.shape
    orders = slot_ref[...] + lax.axis_index("space").astype(F32)
    order_sq = orders * orders
    cosine = lat_ref[0:1, :]
    wrow = lat_ref[1:2, :]
    wcol = jnp.broadcast_to(wrow, (128, width)).T[:, 0:1]
    block = 32

    def degree_block(index, carry):
        p_now, p_prev, e_prev, log_scale = carry
        scale = jnp.exp(log_scale)
        base = index * block
        for inner in range(block):
            degree_int = base + inner
            degree = degree_int.astype(F32)
            active = degree > orders
            square = degree * degree
            ratio = jnp.maximum(square - order_sq, 1.0) / jnp.maximum(4.0 * square - 1.0, 1.0)
            coef = lax.rsqrt(ratio)
            p_next = jnp.where(active, coef * (cosine * p_now - e_prev * p_prev), p_now)
            p_prev = jnp.where(active, p_now, p_prev)
            e_prev = jnp.where(active, ratio * coef, 0.0)
            p_now = p_next
            value = jnp.where(degree >= orders, p_now * scale, 0.0)
            rows = pl.ds(pl.multiple_of(degree_int * groups, groups), groups)
            for part in range(width // 128):
                hold[part, rows, :] = value[:, part * 128 : (part + 1) * 128]
        magnitude = jnp.maximum(jnp.abs(p_now), jnp.abs(p_prev))
        return (p_now / magnitude, p_prev / magnitude, e_prev, log_scale + jnp.log(magnitude))

    ones = jnp.ones((groups, width), F32)
    zeros = jnp.zeros((groups, width), F32)
    lax.fori_loop(0, MODES // block, degree_block, (ones, zeros, zeros, start_ref[...]))

    def spread(g, carry):
        pieces = [
            hold[part, pl.ds(g, MODES, stride=groups), :]
            for part in range(width // 128)
        ]
        value = pieces[0] if len(pieces) == 1 else jnp.concatenate(pieces, 1)
        synth[g] = value.astype(BF16)
        anal[g] = (value * wrow).astype(BF16)
        turned = value.T
        tsynth[g] = turned.astype(BF16)
        tanal[g] = (turned * wcol).astype(BF16)
        return carry

    lax.fori_loop(0, synth.shape[0], spread, 0)


def unpack(src, scratch, q):
    _, devices, span, _ = src.shape
    for a in range(scratch.shape[0]):
        part = src[q, :, :, a * 128 : (a + 1) * 128].astype(F32)
        scratch[a, q * devices * span : (q + 1) * devices * span] = part.reshape(devices * span, 128)


def pack(scratch, dst, q):
    _, devices, span, _ = dst.shape
    for a in range(scratch.shape[0]):
        part = scratch[a, q * devices * span : (q + 1) * devices * span]
        dst[q, :, :, a * 128 : (a + 1) * 128] = part.reshape(devices, span, 128).astype(BF16)


def strided_rows(s, r, devices, span):
    half = span // 2
    start = s // half * (devices * span) + r * half + s % half
    return pl.ds(start, devices, stride=span)


def gather_group(scratch, g, devices, span, per_group, height):
    lat_local = scratch.shape[0]
    rows = []
    for j in range(per_group):
        s = g * per_group + j
        halves = []
        for r in range(2):
            pick = strided_rows(s, r, devices, span)
            parts = [scratch[a, pick, :] for a in range(lat_local)]
            if height > devices * lat_local:
                parts.append(jnp.zeros((height - devices * lat_local, 128), F32))
            halves.append(jnp.concatenate(parts, 0))
        zero = jnp.zeros((height, 256), F32)
        cells = [zero] * per_group
        cells[j] = jnp.concatenate(halves, 1)
        rows.append(cells[0] if per_group == 1 else jnp.concatenate(cells, 1))
    return (rows[0] if per_group == 1 else jnp.concatenate(rows, 0)).astype(BF16)


def scatter_group(value, scratch, g, devices, span, per_group, height):
    lat_local = scratch.shape[0]
    for j in range(per_group):
        s = g * per_group + j
        for r in range(2):
            for a in range(lat_local):
                top = j * height + a * devices
                left = j * 256 + r * 128
                scratch[a, strided_rows(s, r, devices, span), :] = value[
                    top : top + devices, left : left + 128
                ]


def over_groups(groups, sections, section, body):
    pieces = 4
    each = groups // pieces
    share = pieces // sections
    for q in range(section * share, (section + 1) * share):
        first = q * (MODES // pieces)
        lax.fori_loop(q * each, (q + 1) * each, functools.partial(body, first), 0)


def widen(filter_ref, first, copies):
    gain = filter_ref[first:, :].astype(F32)
    return jnp.concatenate([gain] * copies, 1)


def forward_body(per_group, shapes, anal, tsynth, filt, weight, scratch, back):
    _, devices, span, _ = shapes
    height = anal.shape[2] // per_group

    def body(first, g, carry):
        operand = gather_group(scratch, g, devices, span, per_group, height)
        spectrum = jnp.dot(anal[g, first:, :], operand, preferred_element_type=F32).astype(BF16)
        scaled = (spectrum.astype(F32) * widen(filt, first, 2 * per_group)).astype(BF16)
        mixed = [
            jnp.dot(
                scaled[:, j * 256 : (j + 1) * 256], weight[...], preferred_element_type=F32
            ).astype(BF16)
            for j in range(per_group)
        ]
        mixed = mixed[0] if per_group == 1 else jnp.concatenate(mixed, 1)
        value = jnp.dot(tsynth[g, :, first:], mixed, preferred_element_type=F32)
        scatter_group(value, back, g, devices, span, per_group, height)
        return carry

    return body


def backward_body(
    per_group, shapes, anal, synth, tanal, filt, weight, scratch, gscratch, wgrad, fgrad
):
    _, devices, span, _ = shapes
    height = anal.shape[2] // per_group

    def body(first, g, carry):
        operand = gather_group(scratch, g, devices, span, per_group, height)
        goperand = gather_group(gscratch, g, devices, span, per_group, height)
        gain = widen(filt, first, 2)
        outs = []
        spectrum = jnp.dot(anal[g, first:, :], operand, preferred_element_type=F32).astype(BF16)
        gmixed = jnp.dot(synth[g, first:, :], goperand, preferred_element_type=F32).astype(BF16)
        for j in range(per_group):
            lanes = slice(j * 256, (j + 1) * 256)
            spec = spectrum[:, lanes].astype(F32)
            scaled = (spec * gain).astype(BF16)
            gmix = gmixed[:, lanes]
            wgrad[...] += lax.dot_general(
                scaled, gmix, (((0,), (0,)), ((), ())), preferred_element_type=F32
            )
            gscaled = lax.dot_general(
                gmix, weight[...], (((1,), (1,)), ((), ())), preferred_element_type=F32
            )
            term = gscaled * spec
            fgrad[first:, :] += term[:, :128] + term[:, 128:]
            outs.append((gscaled * gain).astype(BF16))
        gspectrum = outs[0] if per_group == 1 else jnp.concatenate(outs, 1)
        value = jnp.dot(tanal[g, :, first:], gspectrum, preferred_element_type=F32)
        scatter_group(value, scratch, g, devices, span, per_group, height)
        return carry

    return body


def fold_gradients(wgrad, fgrad, red):
    half = wgrad.shape[0] // 2
    pieces = [
        (wgrad[:half, :half] + wgrad[half:, half:]) * (1.0 / MODES),
        (wgrad[:half, half:] - wgrad[half:, :half]) * (1.0 / MODES),
        fgrad[...] * 0.125,
    ]
    spare = red.shape[0] * red.shape[1] - 2 * half - MODES
    if spare:
        pieces.append(jnp.zeros((spare, 128), F32))
    red[...] = jnp.concatenate(pieces, 0).reshape(red.shape)


def gelu_slope(field):
    return 0.5 * (1.0 + lax.erf(field * (1.0 / math.sqrt(2.0)))) + field * jnp.exp(
        -0.5 * field * field
    ) * (1.0 / math.sqrt(2.0 * math.pi))


LON_CHUNK = 288


def merged(src, section):
    _, devices, span, width = src.shape
    return src[section].astype(F32).reshape(devices * span, width)


def add_section(ttable, operand, section, field, last):
    count = operand.shape[0]
    lon_count = field.shape[0]

    def grid_rows(q, carry):
        rows = pl.ds(pl.multiple_of(q * LON_CHUNK, LON_CHUNK), LON_CHUNK)
        value = jnp.dot(
            ttable[rows, section * count : (section + 1) * count],
            operand,
            preferred_element_type=F32,
        )
        if section:
            value = value + field[rows, :]
        if last is None:
            field[rows, :] = value
        else:
            last(rows, value)
        return carry

    lax.fori_loop(0, lon_count // LON_CHUNK, grid_rows, 0)


def block_kernel(
    per_group,
    columns, lanes, grid, upstream, slots, start, lats, filt, mix_weight,
    grad, grad_weight, grad_filter,
    weight, total, table, ttable, big, small, tbig, tsmall,
    synth, anal, tsynth, tanal, hold,
    out1, in1, out2, in2, out3, in3, out4, in4,
    scratch, back, field, slope, wgrad, fgrad, red, inbox,
    send1, recv1, send2, recv2, send3, recv3, send4, recv4, rsend, rrecv,
):
    shapes = out1.shape
    sections, devices, span, _ = shapes
    lat_local, lon_count, channels = grid.shape
    groups = synth.shape[0]
    greet(devices)
    weight[:channels, :channels] = mix_weight[0]
    weight[:channels, channels:] = mix_weight[1]
    weight[channels:, :channels] = -mix_weight[1]
    weight[channels:, channels:] = mix_weight[0]
    angles_by_row(columns, lon_count, big, small)
    fill(table, big, small, big.shape[1])

    first = Exchange(out1, in1, send1, recv1)
    wide = jnp.concatenate([grid[a] for a in range(lat_local)], 1)
    for q in range(sections):
        section_product(table, wide, out1, q, False)
        if q == 0:
            await_greetings(devices)
        first.send(q)
    legendre_tables(slots, start, lats, synth, anal, tsynth, tanal, hold)
    angles_by_lane(lanes, lon_count, tbig, tsmall)
    fill(ttable, tbig, tsmall, tbig.shape[1])

    second = Exchange(out2, in2, send2, recv2)
    forward = forward_body(per_group, shapes, anal, tsynth, filt, weight, scratch, back)
    for q in range(sections):
        first.arrive(q)
        unpack(in1, scratch, q)
        over_groups(groups, sections, q, forward)
        pack(back, out2, q)
        second.send(q)

    def gate(rows, value):
        up = jnp.concatenate([upstream[a, rows, :] for a in range(lat_local)], 1)
        slope[rows, :] = (up.astype(F32) * gelu_slope(value)).astype(BF16)

    for q in range(sections):
        second.arrive(q)
        operand = merged(in2, q)
        operand = (operand * alpha_column(q, operand.shape[0], span)).astype(BF16)
        add_section(ttable, operand, q, field, gate if q == sections - 1 else None)

    third = Exchange(out3, in3, send3, recv3)
    for q in range(sections):
        section_product(table, slope[...], out3, q, True)
        third.send(q)

    wgrad[...] = jnp.zeros_like(wgrad)
    fgrad[...] = jnp.zeros_like(fgrad)
    fourth = Exchange(out4, in4, send4, recv4)
    backward = backward_body(
        per_group, shapes, anal, synth, tanal, filt, weight, scratch, back, wgrad, fgrad
    )
    for q in range(sections):
        third.arrive(q)
        unpack(in3, back, q)
        over_groups(groups, sections, q, backward)
        pack(scratch, out4, q)
        if q == 0:
            fourth.send(q)
    fold_gradients(wgrad, fgrad, red)
    reduction = Reduction(red, inbox, total, rsend, rrecv)
    reduction.scatter([functools.partial(fourth.send, q) for q in range(1, sections)])

    def finish(rows, value):
        for a in range(lat_local):
            part = value[:, a * channels : (a + 1) * channels]
            grad[a, rows, :] = (part + upstream[a, rows, :].astype(F32)).astype(BF16)

    hops = len(reduction.hops)
    for step in range(max(hops, sections)):
        copy = reduction.gather(step) if step < hops else None
        if step < sections:
            fourth.arrive(step)
            add_section(
                ttable,
                merged(in4, step).astype(BF16),
                step,
                field,
                finish if step == sections - 1 else None,
            )
        if copy is not None:
            copy.wait()
    sums = total[...].reshape(-1, channels)
    for r in range(2):
        grad_weight[r] = sums[r * channels : (r + 1) * channels]
    grad_filter[...] = sums[2 * channels : 2 * channels + MODES]
    for exchange in (first, second, third, fourth):
        exchange.drain()


def body(grid_in, upstream, mix_weight, degree_filter):
    devices = lax.axis_size("space")
    me = lax.axis_index("space")
    lat_local, lon_count, channels = grid_in.shape
    lat_count = lat_local * devices
    slots = MODES // devices
    sections = sections_of(devices)
    span = 2 * slots // sections
    height = 64 if lat_count <= 64 else -(-lat_count // 128) * 128
    per_group = 128 // height if height < 128 else 1
    width = height * per_group
    groups = slots // per_group
    dims = (sections, devices, span, lat_local * channels)

    lane = np.arange(width)
    within = lane % height
    valid = within < lat_count
    latitude = np.where(valid, within % devices * lat_local + within // devices, 0)
    padded = -(-groups // 8) * 8
    group = np.minimum(np.arange(padded), groups - 1)[:, None]
    slot_orders = ((group * per_group + lane[None, :] // height) * devices).astype(np.float32)
    slot_orders = jnp.asarray(slot_orders)
    angles = latitude_angles(jnp.asarray(latitude), lat_count)
    orders = slot_orders + me.astype(F32)
    start = 0.5 * (jnp.log(2.0 * orders + 1.0) - math.log(2.0))
    start = start + 0.5 * (
        lax.lgamma(2.0 * orders + 1.0) - 2.0 * lax.lgamma(orders + 1.0) - orders * math.log(4.0)
    )
    start = start + orders * jnp.log(jnp.sin(angles))[None, :]
    row = jnp.arange(8)[:, None]
    weights = math.pi / lat_count * jnp.sin(angles) * jnp.asarray(valid.astype(np.float32))
    lats = jnp.where(row == 0, jnp.cos(angles)[None, :], weights[None, :])

    share = -(-(2 * channels + MODES) // (8 * devices)) * 8
    blocks = (devices, share, channels)
    vmem = pltpu.VMEM
    slab = vmem((lat_local, 2 * MODES, 128), F32)
    total_rows = 2 * MODES
    semaphores = pltpu.SemaphoreType.DMA((sections, devices))
    hops = pltpu.SemaphoreType.DMA((2 * devices.bit_length(),))
    return pl.pallas_call(
        functools.partial(block_kernel, per_group),
        out_shape=(
            jax.ShapeDtypeStruct(grid_in.shape, BF16),
            jax.ShapeDtypeStruct(mix_weight.shape, F32),
            jax.ShapeDtypeStruct(degree_filter.shape, F32),
        ),
        scratch_shapes=[
            vmem((2 * channels, 2 * channels), BF16),
            vmem(blocks, F32),
            vmem((total_rows, lon_count), BF16),
            vmem((lon_count, total_rows), BF16),
            vmem((2, total_rows // ROWS, lon_count), F32),
            vmem((2, ROWS, lon_count), F32),
            vmem((2, lon_count // ROWS, total_rows), F32),
            vmem((2, ROWS, total_rows), F32),
            vmem((groups, MODES, width), BF16),
            vmem((groups, MODES, width), BF16),
            vmem((groups, width, MODES), BF16),
            vmem((groups, width, MODES), BF16),
            vmem((width // 128, MODES * padded, 128), F32),
            *[vmem(dims, BF16)] * 8,
            slab,
            slab,
            vmem((lon_count, lat_local * channels), F32),
            vmem((lon_count, lat_local * channels), BF16),
            vmem((2 * channels, 2 * channels), F32),
            vmem((MODES, channels), F32),
            vmem(blocks, F32),
            vmem(blocks, F32),
            *[semaphores] * 8,
            hops,
            hops,
        ],
        compiler_params=params(collective_id=0, has_side_effects=True),
        name="block",
    )(
        *angle_indices(devices, lon_count),
        grid_in,
        upstream,
        slot_orders,
        start,
        lats,
        degree_filter,
        mix_weight,
    )


def solution(mesh):
    return jax.shard_map(
        body,
        mesh=mesh,
        in_specs=(P(("groups", "space"), None, None), P(("groups", "space"), None, None), P(), P()),
        out_specs=(P(("groups", "space"), None, None), P("groups", None, None), P("groups", None)),
        check_vma=False,
    )
```

profile of v0, /device:TPU:0, one launch (start us, length us, event | category | flops | bytes accessed | tf_op | source)
XLA Modules:
  0.0 111.5 jit_solution(2597503864714695471)
XLA Ops:
  0.6 1.3 %broadcast_select_fusion.lats = f32[8,128]{1,0:T(8,128)} fusion(f32[128]{0:T(128)} %constant.95, f32[128]{0:T(128)} %constant.93, pred[8]{0:T(512)(128)(4,1)S(1)} %iota_compare_fusion), kind=kLoop, calls=%fused_computation.76 | loop fusion | flops 1024 | bytes 5128 | tf_op jit(solution)/shard_map/jit(_where)/select_n | solution.py:601
  2.0 1.4 %fusion.16.start = f32[16,128]{1,0:T(8,128)} fusion(f32[16,128]{1,0:T(8,128)} %constant.81.clone.slots, f32[128]{0:T(128)} %constant.92, f32[]{:T(128)S(6)} %convert_element_type.6), kind=kLoop, calls=%fused_computation.24 | loop fusion | flops 235520 | bytes 16900 | tf_op jit(solution)/shard_map/add | solution.py:598
  3.4 104.4 %block.1 = (bf16[3,1440,128]{2,1,0:T(8,128)(2,1)}, f32[2,128,128]{2,1,0:T(8,128)}, f32[512,128]{1,0:T(8,128)}) custom-call(f32[4,32,128]{2,1,0:T(8,128)} %constant.84.clone.columns, f32[2,8,1024]{2,1,0:T(8,128)} %constant.85.clone.lanes, bf16[3,1440,128]{2,1,0:T(8,128)(2,1)} %grid.1, bf16[3,1440,128]{2,1,0:T(8,128)(2,1)} %upstream.1, ...), custom_call_target="tpu_custom_call" | custom-call | tf_op jit(solution)/shard_map/block/pallas_call | solution.py:610
  107.8 0.0 copy-start.1
  107.8 0.0 copy-start
  107.8 2.4 %copy.15 = bf16[3,1440,128]{2,1,0:T(8,128)(2,1)} copy(bf16[3,1440,128]{2,1,0:T(8,128)(2,1)} %get-tuple-element.6) | data formatting | bytes 2211840
  110.2 0.0 copy-done.1
  110.2 0.7 copy.16
  110.8 0.0 copy-done
  110.8 0.7 copy.17
  (1 shorter events, 0.0 us)
Async XLA Ops:
  107.8 2.4 %copy-start.1 = (f32[2,128,128]{2,1,0:T(8,128)S(1)}, f32[2,128,128]{2,1,0:T(8,128)}, u32[]{:S(2)}) copy-start(f32[2,128,128]{2,1,0:T(8,128)} %get-tuple-element.7) | copy-start | bytes 393220
  107.8 3.0 %copy-start = (f32[512,128]{1,0:T(8,128)S(1)}, f32[512,128]{1,0:T(8,128)}, u32[]{:S(2)}) copy-start(f32[512,128]{1,0:T(8,128)} %get-tuple-element.8) | copy-start | bytes 786436
where the time goes:
time: 112 us
  Pallas kernels  104 us (93%)
  local copies, waits for them, and re-layouts  3.72 us (3%)
  other arithmetic  2.77 us (2%)
    pallas_call x1, Pallas kernels, body(): pl.pallas_call(functools.partial(block_kernel, per_group), out_shape=(jax...  104 us
    unnamed x7, local copies, waits for them, and re-layouts  3.72 us

commit v1 on v0

--- a/solution.py
+++ b/solution.py
@@ -56,98 +56,138 @@
     def __init__(self, source, target, send_sem, recv_sem):
         self.source, self.target = source, target
         self.send_sem, self.recv_sem = send_sem, recv_sem
-        self.devices = source.shape[1]
+        self.devices = source.shape[0]
         self.me = lax.axis_index("space")
-
-    def copy(self, section, step):
+        self.started = []
+
+    def copy(self, first, last, step):
         peer = (self.me + step) % self.devices
+        held = pl.ds(first, last - first)
         return remote(
-            self.source.at[section, peer],
-            self.target.at[section, self.me],
-            self.send_sem.at[section, step],
-            self.recv_sem.at[section, step],
+            self.source.at[peer, held],
+            self.target.at[self.me, held],
+            self.send_sem.at[first, step],
+            self.recv_sem.at[first, step],
             peer,
         )
 
-    def send(self, section):
+    def send(self, first, last):
         half = self.devices // 2
 
         def one(index, carry):
             sign = 1 - 2 * (index % 2)
             step = (half + sign * ((index + 1) // 2) + self.devices) % self.devices
-            self.copy(section, step).start()
+            self.copy(first, last, step).start()
             return carry
 
         lax.fori_loop(0, self.devices - 1, one, 0)
-        self.target[section, self.me] = self.source[section, self.me]
-
-    def arrive(self, section):
+        self.started.append((first, last))
+        held = pl.ds(first, last - first)
+        self.target[self.me, held] = self.source[self.me, held]
+
+    def arrive(self, first, last):
         def one(step, carry):
-            self.copy(section, step).wait_recv()
+            self.copy(first, last, step).wait_recv()
             return carry
 
         lax.fori_loop(1, self.devices, one, 0)
 
     def drain(self):
-        for section in range(self.source.shape[0]):
-
-            def one(step, carry, section=section):
-                self.copy(section, step).wait_send()
+        for first, last in self.started:
+
+            def one(step, carry, first=first, last=last):
+                self.copy(first, last, step).wait_send()
                 return carry
 
             lax.fori_loop(1, self.devices, one, 0)
 
 
+def radices_of(devices):
+    radices = []
+    while devices > 1:
+        radix = 8 if devices % 8 == 0 and radices else 2
+        radix = radix if devices % radix == 0 else devices
+        radices.append(radix)
+        devices //= radix
+    return radices
+
+
 class Reduction:
-    def __init__(self, red, inbox, total, send_sem, recv_sem):
-        self.red, self.inbox, self.total = red, inbox, total
+    def __init__(self, red, stage, inbox, total, send_sem, recv_sem):
+        self.red, self.stage, self.inbox, self.total = red, stage, inbox, total
         self.send_sem, self.recv_sem = send_sem, recv_sem
-        devices = red.shape[0]
-        me = lax.axis_index("space")
-        self.hops = []
-        base = me * 0
+        count = red.shape[0]
+        self.me = lax.axis_index("space")
+        self.levels = []
+        base = self.me * 0
         stride = 1
-        while stride < devices:
-            half = devices // (2 * stride)
-            bit = me // stride % 2
-            keep, give = base + bit * half, base + (1 - bit) * half
-            self.hops.append((half, keep, give, me + (1 - 2 * bit) * stride))
-            base = keep
-            stride *= 2
+        offset = 0
+        for radix in radices_of(count):
+            count //= radix
+            digit = self.me // stride % radix
+            self.levels.append((radix, stride, digit, count, base, offset))
+            base = base + digit * count
+            offset += (radix - 1) * count
+            stride *= radix
         self.base = base
 
-    def scatter(self, held):
-        count = len(self.hops)
-        early = max(1, len(held) - 2) if held else 0
-        for send in held[:early]:
-            send()
-        late = held[early:]
-        for t, (half, keep, give, partner) in enumerate(self.hops):
-            copy = remote(
-                self.red.at[pl.ds(give, half)],
-                self.inbox.at[pl.ds(half, half)],
-                self.send_sem.at[t],
-                self.recv_sem.at[t],
-                partner,
+    def scatter_copies(self, level):
+        radix, stride, digit, count, base, offset = self.levels[level]
+        span = pl.ds(base, radix * count)
+        self.stage[span] = self.red[span].astype(BF16)
+        copies = []
+        for k in range(1, radix):
+            other = (digit + k) % radix
+            copies.append(
+                remote(
+                    self.stage.at[pl.ds(base + other * count, count)],
+                    self.inbox.at[pl.ds(offset + (k - 1) * count, count)],
+                    self.send_sem.at[0, level, k],
+                    self.recv_sem.at[0, level, k],
+                    self.me + (other - digit) * stride,
+                )
             )
-            copy.start()
-            index = t - (count - len(late))
-            if index >= 0:
-                late[index]()
+        return copies
+
+    def scatter_end(self, level, copies):
+        radix, _, digit, count, base, offset = self.levels[level]
+        for copy in copies:
             copy.wait()
-            self.red[pl.ds(keep, half)] += self.inbox[half : 2 * half]
-        self.total[pl.ds(self.base, 1)] = self.red[pl.ds(self.base, 1)]
-
-    def gather(self, index):
-        count = len(self.hops)
-        t = count - 1 - index
-        half, keep, _, partner = self.hops[t]
-        block = self.total.at[pl.ds(keep, half)]
-        copy = remote(
-            block, block, self.send_sem.at[count + t], self.recv_sem.at[count + t], partner
-        )
-        copy.start()
-        return copy
+        keep = pl.ds(base + digit * count, count)
+        value = self.red[keep]
+        for k in range(1, radix):
+            low = offset + (k - 1) * count
+            value = value + self.inbox[low : low + count].astype(F32)
+        if level == len(self.levels) - 1:
+            self.total[keep] = value.astype(BF16)
+        else:
+            self.red[keep] = value
+
+    def gather_copies(self, level):
+        radix, stride, digit, count, base, _ = self.levels[level]
+        block = self.total.at[pl.ds(base + digit * count, count)]
+        copies = []
+        for k in range(1, radix):
+            other = (digit + k) % radix
+            copies.append(
+                remote(
+                    block,
+                    block,
+                    self.send_sem.at[1, level, k],
+                    self.recv_sem.at[1, level, k],
+                    self.me + (other - digit) * stride,
+                )
+            )
+        return copies
+
+    def gather_end(self, level, copies):
+        for copy in copies:
+            copy.wait()
+
+    def steps(self):
+        count = len(self.levels)
+        steps = [(self.scatter_copies, self.scatter_end, t) for t in range(count)]
+        return steps + [(self.gather_copies, self.gather_end, t) for t in reversed(range(count))]
 
 
 def sections_of(devices):
@@ -212,13 +252,13 @@
     small[1] = cosine_of(phase + 0.75 * lon_count, lon_count) * factor
 
 
-def fill(dst, big, small, count):
+def fill(dst, big, small, first, last):
     def step(h, carry):
         value = big[0, pl.ds(h, 1), :] * small[0] - big[1, pl.ds(h, 1), :] * small[1]
         dst[pl.ds(pl.multiple_of(h * ROWS, ROWS), ROWS), :] = value.astype(BF16)
         return carry
 
-    lax.fori_loop(0, count, step, 0)
+    lax.fori_loop(first, last, step, 0)
 
 
 def alpha_column(section, rows, span):
@@ -228,17 +268,19 @@
     return alpha[:, 0:1]
 
 
-def section_product(table, wide, out, section, scaled):
-    _, devices, span, width = out.shape
+def section_product(table, wide, out, section, lanes, scaled):
+    devices, _, span, width = out.shape
     count = devices * span
     chunk = 256
     each = chunk // span
     for q in range(count // chunk):
         first = section * count + q * chunk
-        value = jnp.dot(table[first : first + chunk, :], wide, preferred_element_type=F32)
+        value = jnp.dot(
+            table[first : first + chunk, :], wide[:, lanes], preferred_element_type=F32
+        )
         if scaled:
             value = value * (alpha_column(0, chunk, span) if first == 0 else 2.0)
-        out[section, q * each : (q + 1) * each] = value.astype(BF16).reshape(each, span, width)
+        out[q * each : (q + 1) * each, section] = value.astype(BF16).reshape(each, span, width)
 
 
 def legendre_tables(
@@ -294,18 +336,24 @@
     lax.fori_loop(0, synth.shape[0], spread, 0)
 
 
-def unpack(src, scratch, q):
-    _, devices, span, _ = src.shape
-    for a in range(scratch.shape[0]):
-        part = src[q, :, :, a * 128 : (a + 1) * 128].astype(F32)
-        scratch[a, q * devices * span : (q + 1) * devices * span] = part.reshape(devices * span, 128)
-
-
-def pack(scratch, dst, q):
-    _, devices, span, _ = dst.shape
-    for a in range(scratch.shape[0]):
-        part = scratch[a, q * devices * span : (q + 1) * devices * span]
-        dst[q, :, :, a * 128 : (a + 1) * 128] = part.reshape(devices, span, 128).astype(BF16)
+def unpack(sources, parts, scratch, q):
+    for src, (low, high) in zip(sources, parts):
+        devices, _, span, _ = src.shape
+        for a in range(low, high):
+            part = src[:, q, :, (a - low) * 128 : (a - low + 1) * 128].astype(F32)
+            scratch[a, q * devices * span : (q + 1) * devices * span] = part.reshape(
+                devices * span, 128
+            )
+
+
+def pack(scratch, targets, parts, q):
+    for dst, (low, high) in zip(targets, parts):
+        devices, _, span, _ = dst.shape
+        for a in range(low, high):
+            part = scratch[a, q * devices * span : (q + 1) * devices * span]
+            dst[:, q, :, (a - low) * 128 : (a - low + 1) * 128] = part.reshape(
+                devices, span, 128
+            ).astype(BF16)
 
 
 def strided_rows(s, r, devices, span):
@@ -361,7 +409,7 @@
 
 
 def forward_body(per_group, shapes, anal, tsynth, filt, weight, scratch, back):
-    _, devices, span, _ = shapes
+    devices, _, span, _ = shapes
     height = anal.shape[2] // per_group
 
     def body(first, g, carry):
@@ -385,7 +433,7 @@
 def backward_body(
     per_group, shapes, anal, synth, tanal, filt, weight, scratch, gscratch, wgrad, fgrad
 ):
-    _, devices, span, _ = shapes
+    devices, _, span, _ = shapes
     height = anal.shape[2] // per_group
 
     def body(first, g, carry):
@@ -439,132 +487,252 @@
 LON_CHUNK = 288
 
 
-def merged(src, section):
-    _, devices, span, width = src.shape
-    return src[section].astype(F32).reshape(devices * span, width)
-
-
-def add_section(ttable, operand, section, field, last):
+def merged(src, first, last, scaled):
+    devices, _, span, width = src.shape
+    pieces = []
+    for q in range(first, last):
+        value = src[:, q].astype(F32).reshape(devices * span, width)
+        if scaled:
+            value = value * alpha_column(q, devices * span, span)
+        pieces.append(value.astype(BF16))
+    return pieces[0] if len(pieces) == 1 else jnp.concatenate(pieces, 0)
+
+
+def add_sections(ttable, operand, first, field, lanes, last):
     count = operand.shape[0]
     lon_count = field.shape[0]
 
     def grid_rows(q, carry):
         rows = pl.ds(pl.multiple_of(q * LON_CHUNK, LON_CHUNK), LON_CHUNK)
         value = jnp.dot(
-            ttable[rows, section * count : (section + 1) * count],
-            operand,
-            preferred_element_type=F32,
+            ttable[rows, first : first + count], operand, preferred_element_type=F32
         )
-        if section:
-            value = value + field[rows, :]
+        if first:
+            value = value + field[rows, lanes]
         if last is None:
-            field[rows, :] = value
+            field[rows, lanes] = value
         else:
-            last(rows, value)
+            last(q, rows, value)
         return carry
 
     lax.fori_loop(0, lon_count // LON_CHUNK, grid_rows, 0)
+
+
+def lat_parts(lat_local):
+    tail = max(1, lat_local // 3)
+    if lat_local <= tail:
+        return [(0, lat_local)]
+    return [(0, lat_local - tail), (lat_local - tail, lat_local)]
+
+
+def lane_slice(part):
+    return slice(part[0] * 128, part[1] * 128)
 
 
 def block_kernel(
     per_group,
-    columns, lanes, grid, upstream, slots, start, lats, filt, mix_weight,
-    grad, grad_weight, grad_filter,
+    columns_hbm, lanes_hbm, grid_hbm, upstream_hbm, slots_hbm, start_hbm, lats_hbm, filt_hbm, mix_hbm,
+    grad_hbm, sums_hbm,
+    columns, lanes, grid, upstream, slots, start, lats, filt, mix_weight, grad,
     weight, total, table, ttable, big, small, tbig, tsmall,
     synth, anal, tsynth, tanal, hold,
-    out1, in1, out2, in2, out3, in3, out4, in4,
-    scratch, back, field, slope, wgrad, fgrad, red, inbox,
-    send1, recv1, send2, recv2, send3, recv3, send4, recv4, rsend, rrecv,
+    scratch, back, field, slope, wgrad, fgrad, red, stage, inbox,
+    rsend, rrecv, lsem, osem,
+    *buffers,
 ):
-    shapes = out1.shape
-    sections, devices, span, _ = shapes
-    lat_local, lon_count, channels = grid.shape
+    lat_local = grid_hbm.shape[0]
+    parts = lat_parts(lat_local)
+    whole = [(0, lat_local)]
+    split = len(parts)
+    exchanges = [Exchange(*buffers[k : k + 4]) for k in range(0, len(buffers), 4)]
+    first, fourth = exchanges[:2]
+    second, third = exchanges[2 : 2 + split], exchanges[2 + split :]
+    shapes = first.source.shape
+    devices, sections, span, _ = shapes
+    halves = [(0, sections // 2), (sections // 2, sections)] if sections > 1 else [(0, 1)]
+    lat_local, lon_count, channels = grid_hbm.shape
     groups = synth.shape[0]
+    me = lax.axis_index("space")
     greet(devices)
+
+    loads = {}
+
+    def load(name, src, dst):
+        copy = pltpu.make_async_copy(src, dst, lsem.at[len(loads)])
+        copy.start()
+        loads[name] = copy
+
+    load("columns", columns_hbm, columns)
+    for a in range(lat_local):
+        load(("grid", a), grid_hbm.at[a], grid.at[:, a * 128 : (a + 1) * 128])
+    load("slots", slots_hbm, slots)
+    load("start", start_hbm.at[me], start)
+    load("lats", lats_hbm, lats)
+    load("filt", filt_hbm, filt)
+    load("mix", mix_hbm, mix_weight)
+    load("lanes", lanes_hbm, lanes)
+    for a in range(lat_local):
+        load(("up", a), upstream_hbm.at[a], upstream.at[:, a * 128 : (a + 1) * 128])
+
+    everything = slice(0, lat_local * 128)
+    loads["columns"].wait()
+    angles_by_row(columns, lon_count, big, small)
+    share = big.shape[1] // sections
+    for q in range(sections):
+        fill(table, big, small, q * share, (q + 1) * share)
+        if q == 0:
+            for a in range(lat_local):
+                loads["grid", a].wait()
+        section_product(table, grid, first.source, q, everything, False)
+        if q == 0:
+            await_greetings(devices)
+        first.send(q, q + 1)
+    for name in ("slots", "start", "lats", "filt", "mix", "lanes"):
+        loads[name].wait()
     weight[:channels, :channels] = mix_weight[0]
     weight[:channels, channels:] = mix_weight[1]
     weight[channels:, :channels] = -mix_weight[1]
     weight[channels:, channels:] = mix_weight[0]
-    angles_by_row(columns, lon_count, big, small)
-    fill(table, big, small, big.shape[1])
-
-    first = Exchange(out1, in1, send1, recv1)
-    wide = jnp.concatenate([grid[a] for a in range(lat_local)], 1)
-    for q in range(sections):
-        section_product(table, wide, out1, q, False)
-        if q == 0:
-            await_greetings(devices)
-        first.send(q)
     legendre_tables(slots, start, lats, synth, anal, tsynth, tanal, hold)
+
+    forward = forward_body(per_group, shapes, anal, tsynth, filt, weight, scratch, back)
+    for low, high in halves:
+        for q in range(low, high):
+            first.arrive(q, q + 1)
+            unpack([first.target], whole, scratch, q)
+            over_groups(groups, sections, q, forward)
+            pack(back, [exchange.source for exchange in second], parts, q)
+        second[0].send(low, high)
+    for exchange in second[1:]:
+        exchange.send(0, sections)
     angles_by_lane(lanes, lon_count, tbig, tsmall)
-    fill(ttable, tbig, tsmall, tbig.shape[1])
-
-    second = Exchange(out2, in2, send2, recv2)
-    forward = forward_body(per_group, shapes, anal, tsynth, filt, weight, scratch, back)
-    for q in range(sections):
-        first.arrive(q)
-        unpack(in1, scratch, q)
-        over_groups(groups, sections, q, forward)
-        pack(back, out2, q)
-        second.send(q)
-
-    def gate(rows, value):
-        up = jnp.concatenate([upstream[a, rows, :] for a in range(lat_local)], 1)
-        slope[rows, :] = (up.astype(F32) * gelu_slope(value)).astype(BF16)
-
-    for q in range(sections):
-        second.arrive(q)
-        operand = merged(in2, q)
-        operand = (operand * alpha_column(q, operand.shape[0], span)).astype(BF16)
-        add_section(ttable, operand, q, field, gate if q == sections - 1 else None)
-
-    third = Exchange(out3, in3, send3, recv3)
-    for q in range(sections):
-        section_product(table, slope[...], out3, q, True)
-        third.send(q)
+    fill(ttable, tbig, tsmall, 0, tbig.shape[1])
+    for a in range(lat_local):
+        loads["up", a].wait()
+
+    def gate(where, q, rows, value):
+        up = upstream[rows, where].astype(F32)
+        slope[rows, where] = (up * gelu_slope(value)).astype(BF16)
+
+    for p, part in enumerate(parts):
+        where = lane_slice(part)
+        close = functools.partial(gate, where)
+        for low, high in halves if p == 0 else [(0, sections)]:
+            second[p].arrive(low, high)
+            operand = merged(second[p].target, low, high, True)
+            last = close if high == sections else None
+            add_sections(ttable, operand, low * devices * span, field, where, last)
+        for low, high in halves:
+            for q in range(low, high):
+                section_product(table, slope, third[p].source, q, where, True)
+            if p == 0 and low == 0 or split == 1:
+                third[p].send(low, high)
+            if p == split - 1 and p > 0:
+                for exchange in third if low else third[1:]:
+                    exchange.send(low, high)
 
     wgrad[...] = jnp.zeros_like(wgrad)
     fgrad[...] = jnp.zeros_like(fgrad)
-    fourth = Exchange(out4, in4, send4, recv4)
     backward = backward_body(
         per_group, shapes, anal, synth, tanal, filt, weight, scratch, back, wgrad, fgrad
     )
-    for q in range(sections):
-        third.arrive(q)
-        unpack(in3, back, q)
-        over_groups(groups, sections, q, backward)
-        pack(scratch, out4, q)
-        if q == 0:
-            fourth.send(q)
+    for low, high in halves:
+        for exchange in third:
+            exchange.arrive(low, high)
+        for q in range(low, high):
+            unpack([exchange.target for exchange in third], parts, back, q)
+            over_groups(groups, sections, q, backward)
+            pack(scratch, [fourth.source], whole, q)
+            if low == 0 and sections > 1:
+                fourth.send(q, q + 1)
     fold_gradients(wgrad, fgrad, red)
-    reduction = Reduction(red, inbox, total, rsend, rrecv)
-    reduction.scatter([functools.partial(fourth.send, q) for q in range(1, sections)])
-
-    def finish(rows, value):
+    reduction = Reduction(red, stage, inbox, total, rsend, rrecv)
+
+    def out_copy(q, a, rows):
+        return pltpu.make_async_copy(
+            grad.at[rows, a * 128 : (a + 1) * 128], grad_hbm.at[a, rows, :], osem.at[q, a]
+        )
+
+    def finish(q, rows, value):
+        grad[rows, :] = (value + upstream[rows, :].astype(F32)).astype(BF16)
         for a in range(lat_local):
-            part = value[:, a * channels : (a + 1) * channels]
-            grad[a, rows, :] = (part + upstream[a, rows, :].astype(F32)).astype(BF16)
-
-    hops = len(reduction.hops)
-    for step in range(max(hops, sections)):
-        copy = reduction.gather(step) if step < hops else None
-        if step < sections:
-            fourth.arrive(step)
-            add_section(
-                ttable,
-                merged(in4, step).astype(BF16),
-                step,
-                field,
-                finish if step == sections - 1 else None,
+            out_copy(q, a, rows).start()
+
+    def tail(low, high):
+        fourth.arrive(low, high)
+        operand = merged(fourth.target, low, high, False)
+        last = finish if high == sections else None
+        add_sections(ttable, operand, low * devices * span, field, everything, last)
+
+    steps = reduction.steps()
+    middle = len(steps) // 2
+    held = list(range(*halves[-1]))
+    sends = {q: min(middle - 1 + k, middle) for k, q in enumerate(held)}
+    places = {q: min(middle - 1 + q, len(steps) - 1) for q in range(sections - 1)}
+    for index, (begin, end, level) in enumerate(steps):
+        copies = begin(level)
+        for copy in copies:
+            copy.start()
+        for q in held:
+            if sends[q] == index:
+                fourth.send(q, q + 1)
+        for q, place in places.items():
+            if place == index:
+                tail(q, q + 1)
+        end(level, copies)
+    tail(sections - 1, sections)
+    red[...] = total[...].astype(F32)
+    sums_copy = pltpu.make_async_copy(red, sums_hbm, lsem.at[len(loads)])
+    sums_copy.start()
+    for exchange in exchanges:
+        exchange.drain()
+    for q in range(lon_count // LON_CHUNK):
+        rows = pl.ds(q * LON_CHUNK, LON_CHUNK)
+        for a in range(lat_local):
+            out_copy(q, a, rows).wait()
+    sums_copy.wait()
+
+
+def publish_kernel(grad_in, sums_in, grad, weight, filt, grad_v, sums_v, isem, osem):
+    lat_local = grad_in.shape[0]
+    pulls = [
+        pltpu.make_async_copy(grad_in.at[a], grad_v.at[a], isem.at[a]) for a in range(lat_local)
+    ]
+    pulls.append(pltpu.make_async_copy(sums_in, sums_v, isem.at[lat_local]))
+    for copy in pulls:
+        copy.start()
+    pushes = []
+    for a in range(lat_local):
+        pulls[a].wait()
+        pushes.append(pltpu.make_async_copy(grad_v.at[a], grad.at[a], osem.at[a]))
+        pushes[-1].start()
+    pulls[-1].wait()
+    rows = weight.shape[1]
+    for r in range(weight.shape[0]):
+        pushes.append(
+            pltpu.make_async_copy(
+                sums_v.at[pl.ds(r * rows, rows)], weight.at[r], osem.at[lat_local + r]
             )
-        if copy is not None:
-            copy.wait()
-    sums = total[...].reshape(-1, channels)
-    for r in range(2):
-        grad_weight[r] = sums[r * channels : (r + 1) * channels]
-    grad_filter[...] = sums[2 * channels : 2 * channels + MODES]
-    for exchange in (first, second, third, fourth):
-        exchange.drain()
+        )
+    pushes.append(
+        pltpu.make_async_copy(
+            sums_v.at[pl.ds(2 * rows, filt.shape[0])], filt, osem.at[lat_local + weight.shape[0]]
+        )
+    )
+    for copy in pushes[lat_local:]:
+        copy.start()
+    for copy in pushes:
+        copy.wait()
+
+
+def order_logs(devices, group_orders, sines):
+    scale = []
+    for m in range(MODES):
+        value = 0.5 * (math.log(2.0 * m + 1.0) - math.log(2.0))
+        value += 0.5 * (math.lgamma(2.0 * m + 1.0) - 2.0 * math.lgamma(m + 1.0) - m * math.log(4.0))
+        scale.append(value)
+    orders = group_orders[None] + np.arange(devices)[:, None, None]
+    return (np.array(scale)[orders] + orders * np.log(sines)[None, None, :]).astype(np.float32)
 
 
 def body(grid_in, upstream, mix_weight, degree_filter):
@@ -579,7 +747,7 @@
     per_group = 128 // height if height < 128 else 1
     width = height * per_group
     groups = slots // per_group
-    dims = (sections, devices, span, lat_local * channels)
+    dims = (devices, sections, span)
 
     lane = np.arange(width)
     within = lane % height
@@ -587,36 +755,52 @@
     latitude = np.where(valid, within % devices * lat_local + within // devices, 0)
     padded = -(-groups // 8) * 8
     group = np.minimum(np.arange(padded), groups - 1)[:, None]
-    slot_orders = ((group * per_group + lane[None, :] // height) * devices).astype(np.float32)
-    slot_orders = jnp.asarray(slot_orders)
-    angles = latitude_angles(jnp.asarray(latitude), lat_count)
-    orders = slot_orders + me.astype(F32)
-    start = 0.5 * (jnp.log(2.0 * orders + 1.0) - math.log(2.0))
-    start = start + 0.5 * (
-        lax.lgamma(2.0 * orders + 1.0) - 2.0 * lax.lgamma(orders + 1.0) - orders * math.log(4.0)
+    group_orders = (group * per_group + lane[None, :] // height) * devices
+    slot_orders = jnp.asarray(group_orders.astype(np.float32))
+    angles = math.pi * (latitude + 0.5) / lat_count
+    start = jnp.asarray(order_logs(devices, group_orders, np.sin(angles)))
+    weights = math.pi / lat_count * np.sin(angles) * valid
+    lats = np.stack([np.cos(angles)] + [weights] * 7).astype(np.float32)
+    columns, lanes = angle_indices(devices, lon_count)
+    operands = (
+        columns, lanes, grid_in, upstream, slot_orders, start, jnp.asarray(lats), degree_filter, mix_weight,
     )
-    start = start + orders * jnp.log(jnp.sin(angles))[None, :]
-    row = jnp.arange(8)[:, None]
-    weights = math.pi / lat_count * jnp.sin(angles) * jnp.asarray(valid.astype(np.float32))
-    lats = jnp.where(row == 0, jnp.cos(angles)[None, :], weights[None, :])
-
-    share = -(-(2 * channels + MODES) // (8 * devices)) * 8
+
+    share = -(-(2 * channels + MODES) // (16 * devices)) * 16
     blocks = (devices, share, channels)
     vmem = pltpu.VMEM
     slab = vmem((lat_local, 2 * MODES, 128), F32)
     total_rows = 2 * MODES
+    wide = lat_local * channels
     semaphores = pltpu.SemaphoreType.DMA((sections, devices))
-    hops = pltpu.SemaphoreType.DMA((2 * devices.bit_length(),))
-    return pl.pallas_call(
+    buffers = []
+    for low, high in [(0, lat_local)] * 2 + lat_parts(lat_local) * 2:
+        block = vmem((*dims, (high - low) * channels), BF16)
+        buffers += [block, block, semaphores, semaphores]
+    levels = radices_of(devices)
+    hops = pltpu.SemaphoreType.DMA((2, len(levels), max(levels)))
+    anywhere = pl.BlockSpec(memory_space=pl.ANY)
+    grad, sums = pl.pallas_call(
         functools.partial(block_kernel, per_group),
         out_shape=(
             jax.ShapeDtypeStruct(grid_in.shape, BF16),
-            jax.ShapeDtypeStruct(mix_weight.shape, F32),
-            jax.ShapeDtypeStruct(degree_filter.shape, F32),
+            jax.ShapeDtypeStruct(blocks, F32),
         ),
+        in_specs=[anywhere] * len(operands),
+        out_specs=(anywhere, anywhere),
         scratch_shapes=[
+            vmem(columns.shape, F32),
+            vmem(lanes.shape, F32),
+            vmem((lon_count, wide), BF16),
+            vmem((lon_count, wide), BF16),
+            vmem(slot_orders.shape, F32),
+            vmem(start.shape[1:], F32),
+            vmem(lats.shape, F32),
+            vmem(degree_filter.shape, BF16),
+            vmem(mix_weight.shape, BF16),
+            vmem((lon_count, wide), BF16),
             vmem((2 * channels, 2 * channels), BF16),
-            vmem(blocks, F32),
+            vmem(blocks, BF16),
             vmem((total_rows, lon_count), BF16),
             vmem((lon_count, total_rows), BF16),
             vmem((2, total_rows // ROWS, lon_count), F32),
@@ -628,31 +812,42 @@
             vmem((groups, width, MODES), BF16),
             vmem((groups, width, MODES), BF16),
             vmem((width // 128, MODES * padded, 128), F32),
-            *[vmem(dims, BF16)] * 8,
             slab,
             slab,
-            vmem((lon_count, lat_local * channels), F32),
-            vmem((lon_count, lat_local * channels), BF16),
+            vmem((lon_count, wide), F32),
+            vmem((lon_count, wide), BF16),
             vmem((2 * channels, 2 * channels), F32),
             vmem((MODES, channels), F32),
             vmem(blocks, F32),
-            vmem(blocks, F32),
-            *[semaphores] * 8,
+            vmem(blocks, BF16),
+            vmem(blocks, BF16),
             hops,
             hops,
+            pltpu.SemaphoreType.DMA((16 + 2 * lat_local,)),
+            pltpu.SemaphoreType.DMA((lon_count // LON_CHUNK, lat_local)),
+            *buffers,
         ],
         compiler_params=params(collective_id=0, has_side_effects=True),
         name="block",
-    )(
-        *angle_indices(devices, lon_count),
-        grid_in,
-        upstream,
-        slot_orders,
-        start,
-        lats,
-        degree_filter,
-        mix_weight,
-    )
+    )(*operands)
+    flat = sums.reshape(devices * share, channels)
+    return pl.pallas_call(
+        publish_kernel,
+        out_shape=(
+            jax.ShapeDtypeStruct(grid_in.shape, BF16),
+            jax.ShapeDtypeStruct(mix_weight.shape, F32),
+            jax.ShapeDtypeStruct(degree_filter.shape, F32),
+        ),
+        in_specs=[anywhere, anywhere],
+        out_specs=(anywhere,) * 3,
+        scratch_shapes=[
+            vmem(grid_in.shape, BF16),
+            vmem(flat.shape, F32),
+            pltpu.SemaphoreType.DMA((lat_local + 1,)),
+            pltpu.SemaphoreType.DMA((lat_local + 3,)),
+        ],
+        name="publish",
+    )(grad, flat)
 
 
 def solution(mesh):

time: 112 us -> 97 us (0.87)
  Pallas kernels: 104 us -> 96.2 us
  local copies, waits for them, and re-layouts: 3.72 us -> 0 us
  other arithmetic: 2.77 us -> 0 us
    pallas_call x1, Pallas kernels: 104 us -> 94 us  [body(): pl.pallas_call(functools.partial(block_kernel, per_group), out_shape=(jax...]
    unnamed x7 -> x0, local copies, waits for them, and re-layouts: 3.72 us -> none
    pallas_call x0 -> x1, Pallas kernels: none -> 2.18 us  [body(): pl.pallas_call(publish_kernel, out_shape=(jax.ShapeDtypeStruct(grid_in.sh...]
    add x1 -> x0, other arithmetic: 1.42 us -> none  [body(): start = start + orders * jnp.log(jnp.sin(angles))[None, :]]
    select_n x1 -> x0, other arithmetic: 1.34 us -> none  [body(): lats = jnp.where(row == 0, jnp.cos(angles)[None, :], weights[None, :])]
where the time goes in v1:
time: 97 us; the launch traced here: 96.9 us
  Pallas kernels  96.2 us (99%)
    pallas_call x1, Pallas kernels, body(): pl.pallas_call(functools.partial(block_kernel, per_group), out_shape=(jax...  94 us
    pallas_call x1, Pallas kernels, body(): pl.pallas_call(publish_kernel, out_shape=(jax.ShapeDtypeStruct(grid_in.sh...  2.18 us

profile of v1, /device:TPU:0, one launch (start us, length us, event | category | flops | bytes accessed | tf_op | source)
XLA Modules:
  0.0 96.9 jit_solution(16751173552761178078)
XLA Ops:
  0.6 94.0 %block.1 = (bf16[3,1440,128]{2,1,0:T(8,128)(2,1)}, f32[16,48,128]{2,1,0:T(8,128)}) custom-call(f32[4,32,128]{2,1,0:T(8,128)} %constant.12.clone.columns_hbm, f32[2,8,1024]{2,1,0:T(8,128)} %constant.13.clone.lanes_hbm, bf16[3,1440,128]{2,1,0:T(8,128)(2,1)} %grid_hbm.1, bf16[3,1440,128]{2,1,0:T(8,128)(2,1)} %upstream_hbm.1, ...), custom_call_target="tpu_custom_call" | custom-call | tf_op jit(solution)/shard_map/block/pallas_call | solution.py:783
  94.7 2.2 %publish.1 = (bf16[3,1440,128]{2,1,0:T(8,128)(2,1)}, f32[2,128,128]{2,1,0:T(8,128)}, f32[512,128]{1,0:T(8,128)}) custom-call(bf16[3,1440,128]{2,1,0:T(8,128)(2,1)} %get-tuple-element.5.grad_in, f32[768,128]{1,0:T(8,128)} %bitcast.1), custom_call_target="tpu_custom_call" | custom-call | tf_op jit(solution)/shard_map/publish/pallas_call | solution.py:834

commit v2 on v1

--- a/solution.py
+++ b/solution.py
@@ -680,12 +680,13 @@
             if place == index:
                 tail(q, q + 1)
         end(level, copies)
-    tail(sections - 1, sections)
     red[...] = total[...].astype(F32)
     sums_copy = pltpu.make_async_copy(red, sums_hbm, lsem.at[len(loads)])
     sums_copy.start()
-    for exchange in exchanges:
+    for exchange in (first, *second, *third):
         exchange.drain()
+    tail(sections - 1, sections)
+    fourth.drain()
     for q in range(lon_count // LON_CHUNK):
         rows = pl.ds(q * LON_CHUNK, LON_CHUNK)
         for a in range(lat_local):

time: 97 us -> 96.1 us (level)
  no operation moved by 1% of the time
where the time goes in v2:
time: 96.1 us; the launch traced here: 96 us
  Pallas kernels  95.3 us (99%)
    pallas_call x1, Pallas kernels, body(): pl.pallas_call(functools.partial(block_kernel, per_group), out_shape=(jax...  93.2 us
    pallas_call x1, Pallas kernels, body(): pl.pallas_call(publish_kernel, out_shape=(jax.ShapeDtypeStruct(grid_in.sh...  2.18 us

profile of v2, /device:TPU:0, one launch (start us, length us, event | category | flops | bytes accessed | tf_op | source)
XLA Modules:
  0.0 96.0 jit_solution(6231837030425979287)
XLA Ops:
  0.6 93.2 %block.1 = (bf16[3,1440,128]{2,1,0:T(8,128)(2,1)}, f32[16,48,128]{2,1,0:T(8,128)}) custom-call(f32[4,32,128]{2,1,0:T(8,128)} %constant.12.clone.columns_hbm, f32[2,8,1024]{2,1,0:T(8,128)} %constant.13.clone.lanes_hbm, bf16[3,1440,128]{2,1,0:T(8,128)(2,1)} %grid_hbm.1, bf16[3,1440,128]{2,1,0:T(8,128)(2,1)} %upstream_hbm.1, ...), custom_call_target="tpu_custom_call" | custom-call | tf_op jit(solution)/shard_map/block/pallas_call | solution.py:784
  93.8 2.2 %publish.1 = (bf16[3,1440,128]{2,1,0:T(8,128)(2,1)}, f32[2,128,128]{2,1,0:T(8,128)}, f32[512,128]{1,0:T(8,128)}) custom-call(bf16[3,1440,128]{2,1,0:T(8,128)(2,1)} %get-tuple-element.5.grad_in, f32[768,128]{1,0:T(8,128)} %bitcast.1), custom_call_target="tpu_custom_call" | custom-call | tf_op jit(solution)/shard_map/publish/pallas_call | solution.py:835
